TPU v7x, 32 devices: a whole 2x2x4 slice. The times are simulated.
32 devices in a mesh: groups: 2 (over x), tile: 16 (over z, y, core).
Axes of the slice: x: 2, y: 2, z: 4, core: 2. Of those that a mesh axis runs over, the one named last changes fastest.
Arguments:
- latent_rows: bfloat16 [4096, 256], P(('groups', 'tile')), parts along dimension 0, may hold values from -6 to 6
- line_order: int32 [128], P('groups'), parts along dimension 0, may hold values from 0 to 63, each once
- conv_weight: bfloat16 [3, 3, 3, 256, 128], replicated, may hold values from -0.078125 to 0.078125
- conv_bias: float32 [128], replicated, may hold values from -3 to 3
- blend_table: float32 [4, 8], replicated, may hold values from 0.25 to 4
- blend_ids: int32 [32], P('groups'), parts along dimension 0, may hold values from 0 to 3
Outputs:
- frames: bfloat16 [16, 32, 64, 128], P('groups', None, 'tile'), parts along dimension 0
There are 2 independent parts, one for each index of `groups`. A program takes and returns all parts, laid end to end along the dimension named above; an argument that names none is the same for every part. Nothing has to cross between parts.
Inputs may be any that keep to these rules, and one draw needn't show every extreme that they name: line_order is a permutation of the 64 latent lines.
All inputs are finite; a program needn't handle non-finite values.
Results may differ from a plain program's by a relative error of at most 0.001.
Values may be sent and summed in bfloat16 or wider, within the bound.
A program may use at most 64 MiB of HBM per device.

v0:
```python
import jax
import jax.numpy as jnp
from jax import lax
from jax.sharding import PartitionSpec as P

LT = 4
WD = 2


def from_behind(value, axis, steps):
    count = lax.axis_size(axis)
    initial, last = (max(0, -steps), min(count, count - steps))
    return lax.ppermute(value, axis, [(source, source + steps) for source in range(initial, last)])


def upsample(values):
    values = jnp.repeat(values, 2, axis=0)
    values = jnp.repeat(values, 2, axis=1)
    return jnp.repeat(values, 2, axis=2)


def decode_tile(window, conv_weight, conv_bias):
    upsampled = upsample(window)
    upsampled = jnp.concatenate([upsampled[:1], upsampled[:1], upsampled], axis=0)
    output = lax.conv_general_dilated(
        upsampled[None],
        conv_weight,
        (1, 1, 1),
        [(0, 0), (1, 1), (1, 1)],
        dimension_numbers=("NDHWC", "DHWIO", "NDHWC"),
        preferred_element_type=jnp.float32,
    )[0]
    return jax.nn.silu(output + conv_bias)


def blend_profile(blend_table, blend_ids, tile_at):
    kind_index = lax.dynamic_index_in_dim(blend_ids, tile_at, 0, keepdims=False)
    selector = (jnp.arange(blend_table.shape[0], dtype=jnp.int32) == kind_index).astype(jnp.float32)
    return jnp.sum(selector[:, None] * blend_table, axis=0)


def per_device(latent_rows, line_order, conv_weight, conv_bias, blend_table, blend_ids):
    tile_count = lax.axis_size("tile")
    position = lax.axis_index("tile")
    channels = latent_rows.shape[1]
    lines_dev = latent_rows.shape[0] // (WD * tile_count)
    blocks = latent_rows.reshape(lines_dev, tile_count, WD, channels)
    zero_col = jnp.zeros((lines_dev, 1, 1, channels), latent_rows.dtype)
    lower_cols = jnp.concatenate([zero_col, blocks[:, :-1, -1:]], axis=1)
    upper_cols = jnp.concatenate([blocks[:, 1:, :1], zero_col], axis=1)
    widened = jnp.concatenate([lower_cols, blocks, upper_cols], axis=2)
    received = lax.all_to_all(widened, "tile", split_axis=1, concat_axis=0, tiled=True)
    width_now = WD + 2
    line_count = received.shape[0]
    gathered_rows = received.reshape(line_count, width_now, channels)
    inverse = (
        jnp.zeros((line_count,), jnp.int32)
        .at[line_order]
        .set(jnp.arange(line_count, dtype=jnp.int32))
    )
    latent = gathered_rows[inverse].reshape(LT, line_count // LT, width_now, channels)
    decoded = decode_tile(latent, conv_weight, conv_bias)
    lower_at = jnp.maximum(position - 1, 0)
    upper_at = jnp.minimum(position + 1, tile_count - 1)
    has_lower = (position > 0).astype(jnp.float32)
    has_upper = (position < tile_count - 1).astype(jnp.float32)
    weight_self = blend_profile(blend_table, blend_ids, position)
    weight_lower = blend_profile(blend_table, blend_ids, lower_at)
    weight_upper = blend_profile(blend_table, blend_ids, upper_at)
    weighted = decoded * weight_self[None, None, :, None]
    from_lower = from_behind(weighted[:, :, -2:], "tile", 1)
    from_upper = from_behind(weighted[:, :, :2], "tile", -1)
    blended = weighted[:, :, 2:-2]
    blended = blended.at[:, :, :2].add(from_lower)
    blended = blended.at[:, :, -2:].add(from_upper)
    weight_sum = weight_self[2:-2]
    weight_sum = weight_sum.at[:2].add(has_lower * weight_lower[-2:])
    weight_sum = weight_sum.at[-2:].add(has_upper * weight_upper[:2])
    return (blended / weight_sum[None, None, :, None]).astype(jnp.bfloat16)


def solution(mesh):
    return jax.shard_map(
        per_device,
        mesh=mesh,
        in_specs=(P(("groups", "tile"), None), P("groups"), P(), P(), P(), P("groups")),
        out_specs=P("groups", None, "tile", None),
        check_vma=False,
    )
```

profile of v0, /device:TPU:5, one launch (start us, length us, event | category | flops | bytes accessed | tf_op | source)
XLA Modules:
  0.0 53.6 jit_solution(13139769069828558887)
XLA Ops:
  0.0 1.0 %reshape.160 = bf16[4,16,2,256]{3,2,1,0:T(2,128)(2,1)S(1)} reshape(bf16[128,256]{1,0:T(8,128)(2,1)} %param.14) | data formatting | bytes 131072 | tf_op jit(solution)/shard_map/reshape | solution.py:47
  1.1 0.9 %fusion.6 = bf16[4,16,4,256]{3,2,0,1:T(4,128)(2,1)} fusion(bf16[4,15,1,256]{3,2,0,1:T(2,128)(2,1)S(1)} %get-tuple-element.59, bf16[4,15,1,256]{3,2,0,1:T(2,128)(2,1)S(1)} %get-tuple-element.58, bf16[4,16,2,256]{3,2,1,0:T(2,128)(2,1)S(1)} %reshape.160), kind=kLoop, calls=%fused_computation.15 | loop fusion | flops 655360 | bytes 258048 | tf_op jit(solution)/shard_map/concatenate | solution.py:51
  2.0 6.6 %all-to-all-start = ((bf16[4,16,4,256]{3,2,0,1:T(4,128)(2,1)}), bf16[4,16,4,256]{3,2,0,1:T(4,128)(2,1)S(1)}, u32[]{:S(2)}, u32[]{:S(2)}) async-start(bf16[4,16,4,256]{3,2,0,1:T(4,128)(2,1)} %fusion.6), calls=%async_computation | async-start | bytes 262144 | tf_op jit(solution)/shard_map/all_to_all | solution.py:52
  8.6 1.4 %fusion.12 = (s32[1]{0:T(128)}, s32[1]{0:T(128)}, s32[1]{0:T(128)}) fusion(s32[16]{0:T(128)} %param.19, s32[]{:T(128)S(6)} %max.3, s32[]{:T(128)S(6)} %select_n.16, s32[]{:T(128)S(6)} %select_n.17), kind=kLoop, calls=%fused_computation.33 | loop fusion | bytes 36 | tf_op jit(solution)/shard_map/jit(dynamic_index_in_dim)/dynamic_slice | solution.py:37
  10.1 0.6 %compare_convert_fusion.2 = f32[4]{0:T(128)S(1)} fusion(s32[]{:T(128)} %bitcast.10), kind=kLoop, calls=%fused_computation.26 | loop fusion | flops 8 | bytes 20 | tf_op jit(solution)/shard_map/convert_element_type | solution.py:38
  10.7 1.2 %compare_convert_fusion = (f32[4]{0:T(128)S(1)}, f32[4]{0:T(128)S(1)}) fusion(s32[]{:T(128)} %bitcast.12, s32[]{:T(128)} %bitcast.11), kind=kLoop, calls=%fused_computation.24 | loop fusion | flops 16 | bytes 40 | tf_op jit(solution)/shard_map/convert_element_type | solution.py:38
  11.9 0.8 %multiply_reduce_fusion = (f32[8]{0:T(128)S(1)}, f32[8]{0:T(128)S(1)}, f32[8]{0:T(128)S(1)}) fusion(f32[4,8]{1,0:T(4,128)} %param.18, f32[4]{0:T(128)S(1)} %get-tuple-element.63, f32[4]{0:T(128)S(1)} %compare_convert_fusion.2, f32[4]{0:T(128)S(1)} %get-tuple-element.64), kind=kLoop, calls=%fused_computation.21 | loop fusion | flops 168 | bytes 272 | tf_op jit(solution)/shard_map/reduce_sum | solution.py:39
  12.8 0.7 %compare_select_fusion.1 = s32[64]{0:T(128)S(1)} fusion(s32[64]{0:T(128)} %param.15), kind=kLoop, calls=%fused_computation.20 | loop fusion | flops 192 | bytes 512 | tf_op jit(solution)/shard_map/select_n | solution.py:59
  13.4 0.8 %scatter_custom_fusion = s32[64]{0:T(128)S(1)} fusion(s32[64]{0:T(128)S(1)} %compare_select_fusion.1, s32[64]{0:T(128)S(1)} %iota.18, s32[]{:T(128)} %constant.121.clone.1), kind=kCustom, calls=%fused_computation.29 | custom fusion | bytes 260 | tf_op jit(solution)/shard_map/scatter | solution.py:59
  14.2 0.3 all-to-all-done
  14.5 0.7 %gather_fusion = bf16[64,4,256]{2,1,0:T(4,128)(2,1)S(1)} fusion(bf16[64,4,256]{2,1,0:T(4,128)(2,1)S(1)} %bitcast.24, s32[1024]{0:T(1024)S(1)} %pad_clamp_fusion), kind=kCustom, calls=%fused_computation | custom fusion | bytes 262400 | tf_op jit(solution)/shard_map/gather | solution.py:61
  15.7 1.7 %broadcast_in_dim.41 = bf16[8,32,4,2,256]{4,3,2,1,0:T(2,128)(2,1)} broadcast(bf16[8,32,4,256]{3,2,1,0:T(4,128)(2,1)S(1)} %bitcast.19), dimensions={0,1,2,4} | broadcast | bytes 1572864 | tf_op jit(solution)/shard_map/broadcast_in_dim | solution.py:19
  17.4 1.5 %reshape.165 = bf16[8,32,8,256]{3,2,1,0:T(8,128)(2,1)S(1)} reshape(bf16[8,32,4,2,256]{4,3,2,1,0:T(2,128)(2,1)} %broadcast_in_dim.41) | data formatting | bytes 2097152 | tf_op jit(solution)/shard_map/reshape | solution.py:19
  19.0 20.3 %fusion = f32[1,8,32,8,128]{4,0,3,2,1:T(1,128)S(1)} fusion(bf16[3,3,3,256,128]{4,3,2,1,0:T(8,128)(2,1)S(1)} %copy-done, bf16[1,10,32,8,256]{4,3,2,1,0:T(8,128)(2,1)S(1)} %maximum_bitcast_fusion), kind=kOutput, calls=%fused_computation.2 | convolution fusion | flops 3252682752 | bytes 4128768 | tf_op jit(solution)/shard_map/conv_general_dilated | solution.py:25
  39.3 0.3 multiply_multiply_fusion
  39.6 0.9 %fusion.10 = (f32[8,32,2,128]{3,2,1,0:T(2,128)S(1)}, f32[8,32,2,128]{3,2,1,0:T(2,128)}) fusion(f32[8,32,8,128]{3,2,1,0:T(8,128)S(1)} %multiply_multiply_fusion), kind=kLoop, calls=%fused_computation.31 | loop fusion | bytes 1048576 | tf_op jit(solution)/shard_map/slice | solution.py:72
  40.5 3.1 %collective-permute-start = (f32[8,32,2,128]{3,2,1,0:T(2,128)}, f32[8,32,2,128]{3,2,1,0:T(2,128)S(1)}, u32[]{:S(2)}, u32[]{:S(2)}) collective-permute-start(f32[8,32,2,128]{3,2,1,0:T(2,128)} %get-tuple-element.57), channel_id=1, source_target_pairs={{0,1},{1,2},{2,3},{3,4},{4,5},{5,6},{6,7},{7,8},{8,9},{9,10},{10,1... | collective-permute-start | bytes 786440 | tf_op jit(solution)/shard_map/ppermute | solution.py:13
  43.6 0.2 constant_dynamic-update-slice_fusion
  43.9 1.9 %collective-permute-start.1 = (f32[8,32,2,128]{3,2,1,0:T(2,128)S(1)}, f32[8,32,2,128]{3,2,1,0:T(2,128)S(1)}, u32[]{:S(2)}, u32[]{:S(2)}) collective-permute-start(f32[8,32,2,128]{3,2,1,0:T(2,128)S(1)} %get-tuple-element.56), channel_id=1, source_target_pairs={{1,0},{2,1},{3,2},{4,3},{5,4},{6,5},{7,6},{8,7},{9,8},{10,9},{11,1... | collective-permute-start | bytes 786440 | tf_op jit(solution)/shard_map/ppermute | solution.py:13
  45.8 1.3 %collective-permute-done = f32[8,32,2,128]{3,2,1,0:T(2,128)S(1)} collective-permute-done((f32[8,32,2,128]{3,2,1,0:T(2,128)}, f32[8,32,2,128]{3,2,1,0:T(2,128)S(1)}, u32[]{:S(2)}, u32[]{:S(2)}) %collective-permute-start) | collective-permute-done | bytes 262176 | tf_op jit(solution)/shard_map/ppermute | solution.py:13
  47.1 0.2 fusion.3
  47.4 5.1 %collective-permute-done.1 = f32[8,32,2,128]{3,2,1,0:T(2,128)S(1)} collective-permute-done((f32[8,32,2,128]{3,2,1,0:T(2,128)S(1)}, f32[8,32,2,128]{3,2,1,0:T(2,128)S(1)}, u32[]{:S(2)}, u32[]{:S(2)}) %collective-permute-start.1) | collective-permute-done | bytes 262176 | tf_op jit(solution)/shard_map/ppermute | solution.py:13
  52.5 0.3 fusion.2
  52.8 0.9 %divide_convert_fusion = bf16[8,32,4,128]{3,2,1,0:T(4,128)(2,1)} fusion(f32[8,32,4,128]{3,2,1,0:T(4,128)S(1)} %fusion.2, f32[4]{0:T(128)S(1)} %constant_dynamic-update-slice_fusion), kind=kLoop, calls=%fused_computation.6 | loop fusion | flops 262144 | bytes 786448 | tf_op jit(solution)/shard_map/convert_element_type | solution.py:79
  (18 shorter events, 0.9 us)
Async XLA Ops:
  0.0 18.9 %copy-start = (bf16[3,3,3,256,128]{4,3,2,1,0:T(8,128)(2,1)S(1)}, bf16[3,3,3,256,128]{4,3,2,1,0:T(8,128)(2,1)}, u32[]{:S(2)}) copy-start(bf16[3,3,3,256,128]{4,3,2,1,0:T(8,128)(2,1)} %param.16) | copy-start | bytes 5308420
  2.0 12.5 %all-to-all-start = ((bf16[4,16,4,256]{3,2,0,1:T(4,128)(2,1)}), bf16[4,16,4,256]{3,2,0,1:T(4,128)(2,1)S(1)}, u32[]{:S(2)}, u32[]{:S(2)}) async-start(bf16[4,16,4,256]{3,2,0,1:T(4,128)(2,1)} %fusion.6), calls=%async_computation | async-start | bytes 262144 | tf_op jit(solution)/shard_map/all_to_all | solution.py:52
  19.0 20.3 %copy-start.1 = (f32[128]{0:T(128)S(1)}, f32[128]{0:T(128)}, u32[]{:S(2)}) copy-start(f32[128]{0:T(128)} %param.17) | copy-start | bytes 1540
  40.5 6.7 %collective-permute-start = (f32[8,32,2,128]{3,2,1,0:T(2,128)}, f32[8,32,2,128]{3,2,1,0:T(2,128)S(1)}, u32[]{:S(2)}, u32[]{:S(2)}) collective-permute-start(f32[8,32,2,128]{3,2,1,0:T(2,128)} %get-tuple-element.57), channel_id=1, source_target_pairs={{0,1},{1,2},{2,3},{3,4},{4,5},{5,6},{6,7},{7,8},{8,9},{9,10},{10,1... | collective-permute-start | bytes 786440 | tf_op jit(solution)/shard_map/ppermute | solution.py:13
  43.9 8.6 %collective-permute-start.1 = (f32[8,32,2,128]{3,2,1,0:T(2,128)S(1)}, f32[8,32,2,128]{3,2,1,0:T(2,128)S(1)}, u32[]{:S(2)}, u32[]{:S(2)}) collective-permute-start(f32[8,32,2,128]{3,2,1,0:T(2,128)S(1)} %get-tuple-element.56), channel_id=1, source_target_pairs={{1,0},{2,1},{3,2},{4,3},{5,4},{6,5},{7,6},{8,7},{9,8},{10,9},{11,1... | collective-permute-start | bytes 786440 | tf_op jit(solution)/shard_map/ppermute | solution.py:13
where the time goes:
time: 54 us; the launch traced here: 53.6 us
  matrix products  20.3 us (38%)
  starting transfers between devices  11.6 us (21%)
  local copies, waits for them, and re-layouts  8.63 us (16%)
  waiting for transfers between devices  6.73 us (12%)
  other arithmetic  6.2 us (11%)
    conv_general_dilated x1, matrix products, decode_tile(): lax.conv_general_dilated(upsampled[None], conv_weight, (1, 1, 1), [(0, 0)...  20.3 us
    all_to_all x1, starting transfers between devices, per_device(): lax.all_to_all(widened, 'tile', split_axis=1, concat_axis=0, tiled=True)  6.63 us
    ppermute x2, waiting for transfers between devices, from_behind(): lax.ppermute(value, axis, [(source, source + steps) for source in range(i...  6.41 us
    ppermute x2, starting transfers between devices, from_behind(): lax.ppermute(value, axis, [(source, source + steps) for source in range(i...  4.97 us
    broadcast_in_dim x3, local copies, waits for them, and re-layouts, upsample(): return jnp.repeat(values, 2, axis=2)  1.84 us
    convert_element_type x2, other arithmetic, blend_profile(): (jnp.arange(blend_table.shape[0], dtype=jnp.int32) == kind_index).astype(...  1.83 us
    reshape x1, local copies, waits for them, and re-layouts, upsample(): return jnp.repeat(values, 2, axis=2)  1.47 us
    dynamic_slice x1, local copies, waits for them, and re-layouts, blend_profile(): kind_index = lax.dynamic_index_in_dim(blend_ids, tile_at, 0, keepdims=False)  1.42 us
  transfers between devices with their start and end apart: 3, of which 3 were waited for; matrix products, arithmetic and copies ran while one was open for 11% of the time, Pallas kernels for 0%

commit v1 on v0

--- a/solution.py
+++ b/solution.py
@@ -49,7 +49,10 @@
     lower_cols = jnp.concatenate([zero_col, blocks[:, :-1, -1:]], axis=1)
     upper_cols = jnp.concatenate([blocks[:, 1:, :1], zero_col], axis=1)
     widened = jnp.concatenate([lower_cols, blocks, upper_cols], axis=2)
-    received = lax.all_to_all(widened, "tile", split_axis=1, concat_axis=0, tiled=True)
+    size = lax.axis_size("tile")
+    pieces = jnp.stack(jnp.split(widened, size, axis=1), axis=0)
+    pieces = lax.all_to_all(pieces, "tile", split_axis=0, concat_axis=0)
+    received = jnp.concatenate(pieces, axis=0)
     width_now = WD + 2
     line_count = received.shape[0]
     gathered_rows = received.reshape(line_count, width_now, channels)

time: 54 us -> 63 us (1.17)
  local copies, waits for them, and re-layouts: 8.63 us -> 18.3 us
  other arithmetic: 6.2 us -> 5.54 us
    unnamed x4 -> x19, local copies, waits for them, and re-layouts: 0.01 us -> 9.05 us
    concatenate x1, other arithmetic: 0.91 us -> 0.25 us  [per_device(): widened = jnp.concatenate([lower_cols, blocks, upper_cols], axis=2)]
  transfers between devices with their start and end apart: 3 -> 3, of which waited for: 3 -> 3; matrix products, arithmetic and copies ran while one was open for 11% -> 10% of each run, Pallas kernels for 0% -> 0%
where the time goes in v1:
time: 63 us; the launch traced here: 62.6 us
  matrix products  20.3 us (32%)
  local copies, waits for them, and re-layouts  18.3 us (29%)
  starting transfers between devices  11.6 us (18%)
  waiting for transfers between devices  6.73 us (11%)
  other arithmetic  5.54 us (9%)
    conv_general_dilated x1, matrix products, decode_tile(): lax.conv_general_dilated(upsampled[None], conv_weight, (1, 1, 1), [(0, 0)...  20.3 us
    unnamed x19, local copies, waits for them, and re-layouts  9.05 us
    all_to_all x1, starting transfers between devices, per_device(): pieces = lax.all_to_all(pieces, 'tile', split_axis=0, concat_axis=0)  6.63 us
    ppermute x2, waiting for transfers between devices, from_behind(): lax.ppermute(value, axis, [(source, source + steps) for source in range(i...  6.41 us
    ppermute x2, starting transfers between devices, from_behind(): lax.ppermute(value, axis, [(source, source + steps) for source in range(i...  4.97 us
    broadcast_in_dim x3, local copies, waits for them, and re-layouts, upsample(): return jnp.repeat(values, 2, axis=2)  1.84 us
    convert_element_type x2, other arithmetic, blend_profile(): (jnp.arange(blend_table.shape[0], dtype=jnp.int32) == kind_index).astype(...  1.83 us
    reshape x1, local copies, waits for them, and re-layouts, upsample(): return jnp.repeat(values, 2, axis=2)  1.47 us
  transfers between devices with their start and end apart: 3, of which 3 were waited for; matrix products, arithmetic and copies ran while one was open for 10% of the time, Pallas kernels for 0%

profile of v1, /device:TPU:5, one launch (start us, length us, event | category | flops | bytes accessed | tf_op | source)
XLA Modules:
  0.0 62.6 jit_solution(13643712092157361878)
XLA Ops:
  0.0 1.0 %reshape.156 = bf16[4,16,2,256]{3,2,1,0:T(2,128)(2,1)S(1)} reshape(bf16[128,256]{1,0:T(8,128)(2,1)} %param.14) | data formatting | bytes 131072 | tf_op jit(solution)/shard_map/reshape | solution.py:47
  1.4 0.6 constant_dynamic-update-slice_fusion.15
  3.8 0.6 constant_dynamic-update-slice_fusion.11
  4.4 0.6 constant_dynamic-update-slice_fusion.10
  5.0 0.6 constant_dynamic-update-slice_fusion.9
  5.6 0.6 constant_dynamic-update-slice_fusion.8
  6.2 0.6 constant_dynamic-update-slice_fusion.7
  11.0 6.6 %all-to-all-start = ((bf16[16,4,1,4,256]{4,3,1,2,0:T(4,128)(2,1)}), bf16[16,4,1,4,256]{4,3,1,2,0:T(4,128)(2,1)S(1)}, u32[]{:S(2)}, u32[]{:S(2)}) async-start(bf16[16,4,1,4,256]{4,3,1,2,0:T(4,128)(2,1)} %constant_dynamic-update-slice_fusion), calls=%async_computation | async-start | bytes 262144 | tf_op jit(solution)/shard_map/all_to_all | solution.py:54
  17.6 1.4 %fusion.12 = (s32[1]{0:T(128)}, s32[1]{0:T(128)}, s32[1]{0:T(128)}) fusion(s32[16]{0:T(128)} %param.19, s32[]{:T(128)S(6)} %max.3, s32[]{:T(128)S(6)} %select_n.16, s32[]{:T(128)S(6)} %select_n.17), kind=kLoop, calls=%fused_computation.65 | loop fusion | bytes 36 | tf_op jit(solution)/shard_map/jit(dynamic_index_in_dim)/dynamic_slice | solution.py:37
  19.1 0.6 %compare_convert_fusion.2 = f32[4]{0:T(128)S(1)} fusion(s32[]{:T(128)} %bitcast.24), kind=kLoop, calls=%fused_computation.58 | loop fusion | flops 8 | bytes 20 | tf_op jit(solution)/shard_map/convert_element_type | solution.py:38
  19.7 1.2 %compare_convert_fusion = (f32[4]{0:T(128)S(1)}, f32[4]{0:T(128)S(1)}) fusion(s32[]{:T(128)} %bitcast.26, s32[]{:T(128)} %bitcast.25), kind=kLoop, calls=%fused_computation.56 | loop fusion | flops 16 | bytes 40 | tf_op jit(solution)/shard_map/convert_element_type | solution.py:38
  20.9 0.8 %multiply_reduce_fusion = (f32[8]{0:T(128)S(1)}, f32[8]{0:T(128)S(1)}, f32[8]{0:T(128)S(1)}) fusion(f32[4,8]{1,0:T(4,128)} %param.18, f32[4]{0:T(128)S(1)} %get-tuple-element.63, f32[4]{0:T(128)S(1)} %compare_convert_fusion.2, f32[4]{0:T(128)S(1)} %get-tuple-element.64), kind=kLoop, calls=%fused_computation.53 | loop fusion | flops 168 | bytes 272 | tf_op jit(solution)/shard_map/reduce_sum | solution.py:39
  21.8 0.7 %compare_select_fusion.1 = s32[64]{0:T(128)S(1)} fusion(s32[64]{0:T(128)} %param.15), kind=kLoop, calls=%fused_computation.52 | loop fusion | flops 192 | bytes 512 | tf_op jit(solution)/shard_map/select_n | solution.py:62
  22.4 0.8 %scatter_custom_fusion = s32[64]{0:T(128)S(1)} fusion(s32[64]{0:T(128)S(1)} %compare_select_fusion.1, s32[64]{0:T(128)S(1)} %iota.18, s32[]{:T(128)} %constant.121.clone.1), kind=kCustom, calls=%fused_computation.61 | custom fusion | bytes 260 | tf_op jit(solution)/shard_map/scatter | solution.py:62
  23.5 0.7 %gather_fusion = bf16[64,4,256]{2,1,0:T(4,128)(2,1)S(1)} fusion(bf16[64,4,256]{2,1,0:T(4,128)(2,1)S(1)} %bitcast.114, s32[1024]{0:T(1024)S(1)} %pad_clamp_fusion), kind=kCustom, calls=%fused_computation | custom fusion | bytes 262400 | tf_op jit(solution)/shard_map/gather | solution.py:64
  24.7 1.7 %broadcast_in_dim.41 = bf16[8,32,4,2,256]{4,3,2,1,0:T(2,128)(2,1)} broadcast(bf16[8,32,4,256]{3,2,1,0:T(4,128)(2,1)S(1)} %bitcast.109), dimensions={0,1,2,4} | broadcast | bytes 1572864 | tf_op jit(solution)/shard_map/broadcast_in_dim | solution.py:19
  26.4 1.5 %reshape.160 = bf16[8,32,8,256]{3,2,1,0:T(8,128)(2,1)S(1)} reshape(bf16[8,32,4,2,256]{4,3,2,1,0:T(2,128)(2,1)} %broadcast_in_dim.41) | data formatting | bytes 2097152 | tf_op jit(solution)/shard_map/reshape | solution.py:19
  28.0 20.3 %fusion = f32[1,8,32,8,128]{4,0,3,2,1:T(1,128)S(1)} fusion(bf16[3,3,3,256,128]{4,3,2,1,0:T(8,128)(2,1)S(1)} %copy-done, bf16[1,10,32,8,256]{4,3,2,1,0:T(8,128)(2,1)S(1)} %maximum_bitcast_fusion), kind=kOutput, calls=%fused_computation.2 | convolution fusion | flops 3252682752 | bytes 4128768 | tf_op jit(solution)/shard_map/conv_general_dilated | solution.py:25
  48.6 0.9 %fusion.10 = (f32[8,32,2,128]{3,2,1,0:T(2,128)S(1)}, f32[8,32,2,128]{3,2,1,0:T(2,128)}) fusion(f32[8,32,8,128]{3,2,1,0:T(8,128)S(1)} %multiply_multiply_fusion), kind=kLoop, calls=%fused_computation.63 | loop fusion | bytes 1048576 | tf_op jit(solution)/shard_map/slice | solution.py:75
  49.5 3.1 %collective-permute-start = (f32[8,32,2,128]{3,2,1,0:T(2,128)}, f32[8,32,2,128]{3,2,1,0:T(2,128)S(1)}, u32[]{:S(2)}, u32[]{:S(2)}) collective-permute-start(f32[8,32,2,128]{3,2,1,0:T(2,128)} %get-tuple-element.57), channel_id=1, source_target_pairs={{0,1},{1,2},{2,3},{3,4},{4,5},{5,6},{6,7},{7,8},{8,9},{9,10},{10,1... | collective-permute-start | bytes 786440 | tf_op jit(solution)/shard_map/ppermute | solution.py:13
  52.9 1.9 %collective-permute-start.1 = (f32[8,32,2,128]{3,2,1,0:T(2,128)S(1)}, f32[8,32,2,128]{3,2,1,0:T(2,128)S(1)}, u32[]{:S(2)}, u32[]{:S(2)}) collective-permute-start(f32[8,32,2,128]{3,2,1,0:T(2,128)S(1)} %get-tuple-element.56), channel_id=1, source_target_pairs={{1,0},{2,1},{3,2},{4,3},{5,4},{6,5},{7,6},{8,7},{9,8},{10,9},{11,1... | collective-permute-start | bytes 786440 | tf_op jit(solution)/shard_map/ppermute | solution.py:13
  54.8 1.3 %collective-permute-done = f32[8,32,2,128]{3,2,1,0:T(2,128)S(1)} collective-permute-done((f32[8,32,2,128]{3,2,1,0:T(2,128)}, f32[8,32,2,128]{3,2,1,0:T(2,128)S(1)}, u32[]{:S(2)}, u32[]{:S(2)}) %collective-permute-start) | collective-permute-done | bytes 262176 | tf_op jit(solution)/shard_map/ppermute | solution.py:13
  56.4 5.1 %collective-permute-done.1 = f32[8,32,2,128]{3,2,1,0:T(2,128)S(1)} collective-permute-done((f32[8,32,2,128]{3,2,1,0:T(2,128)S(1)}, f32[8,32,2,128]{3,2,1,0:T(2,128)S(1)}, u32[]{:S(2)}, u32[]{:S(2)}) %collective-permute-start.1) | collective-permute-done | bytes 262176 | tf_op jit(solution)/shard_map/ppermute | solution.py:13
  61.8 0.9 %divide_convert_fusion = bf16[8,32,4,128]{3,2,1,0:T(4,128)(2,1)} fusion(f32[8,32,4,128]{3,2,1,0:T(4,128)S(1)} %fusion.2, f32[4]{0:T(128)S(1)} %constant_dynamic-update-slice_fusion.16), kind=kLoop, calls=%fused_computation.6 | loop fusion | flops 262144 | bytes 786448 | tf_op jit(solution)/shard_map/convert_element_type | solution.py:82
  (34 shorter events, 8.4 us)
Async XLA Ops:
  0.0 27.9 %copy-start = (bf16[3,3,3,256,128]{4,3,2,1,0:T(8,128)(2,1)S(1)}, bf16[3,3,3,256,128]{4,3,2,1,0:T(8,128)(2,1)}, u32[]{:S(2)}) copy-start(bf16[3,3,3,256,128]{4,3,2,1,0:T(8,128)(2,1)} %param.16) | copy-start | bytes 5308420
  11.0 12.5 %all-to-all-start = ((bf16[16,4,1,4,256]{4,3,1,2,0:T(4,128)(2,1)}), bf16[16,4,1,4,256]{4,3,1,2,0:T(4,128)(2,1)S(1)}, u32[]{:S(2)}, u32[]{:S(2)}) async-start(bf16[16,4,1,4,256]{4,3,1,2,0:T(4,128)(2,1)} %constant_dynamic-update-slice_fusion), calls=%async_computation | async-start | bytes 262144 | tf_op jit(solution)/shard_map/all_to_all | solution.py:54
  28.0 20.3 %copy-start.1 = (f32[128]{0:T(128)S(1)}, f32[128]{0:T(128)}, u32[]{:S(2)}) copy-start(f32[128]{0:T(128)} %param.17) | copy-start | bytes 1540
  49.5 6.7 %collective-permute-start = (f32[8,32,2,128]{3,2,1,0:T(2,128)}, f32[8,32,2,128]{3,2,1,0:T(2,128)S(1)}, u32[]{:S(2)}, u32[]{:S(2)}) collective-permute-start(f32[8,32,2,128]{3,2,1,0:T(2,128)} %get-tuple-element.57), channel_id=1, source_target_pairs={{0,1},{1,2},{2,3},{3,4},{4,5},{5,6},{6,7},{7,8},{8,9},{9,10},{10,1... | collective-permute-start | bytes 786440 | tf_op jit(solution)/shard_map/ppermute | solution.py:13
  52.9 8.6 %collective-permute-start.1 = (f32[8,32,2,128]{3,2,1,0:T(2,128)S(1)}, f32[8,32,2,128]{3,2,1,0:T(2,128)S(1)}, u32[]{:S(2)}, u32[]{:S(2)}) collective-permute-start(f32[8,32,2,128]{3,2,1,0:T(2,128)S(1)} %get-tuple-element.56), channel_id=1, source_target_pairs={{1,0},{2,1},{3,2},{4,3},{5,4},{6,5},{7,6},{8,7},{9,8},{10,9},{11,1... | collective-permute-start | bytes 786440 | tf_op jit(solution)/shard_map/ppermute | solution.py:13
